TPU v7x, 32 devices: a whole 2x2x4 slice. The times are simulated.
32 devices in a mesh: ctx: 2 (over y), branch: 4 (over z), head: 4 (over x, core).
Axes of the slice: x: 2, y: 2, z: 4, core: 2. Of those that a mesh axis runs over, the one named last changes fastest.
Arguments:
- queries: bfloat16 [8, 128, 4096], P(('ctx', 'branch'), None, 'head'), may hold values from -320 to 320
- branch_keys: bfloat16 [8, 128, 512], P(('ctx', 'branch'), None, 'head'), may hold values from -12 to 12
- branch_value_rows: bfloat16 [8, 128, 512], P(('ctx', 'branch'), None, 'head'), may hold values from -6 to 6
- trunk_key_rows: bfloat16 [192, 512], P('ctx', 'head'), may hold values from -6 to 6
- trunk_value_rows: bfloat16 [192, 512], P('ctx', 'head'), may hold values from -6 to 6
- attn_out: bfloat16 [8, 128, 4096], P(('ctx', 'branch'), None, 'head'), may hold values from -2 to 2
- out_grad: bfloat16 [8, 128, 4096], P(('ctx', 'branch'), None, 'head'), may hold values from -6 to 6
- block_mask: int32 [8, 1, 3], P(('ctx', 'branch')), may hold values from 0 to 1, as said below
Outputs:
- query_grad: bfloat16 [8, 128, 4096], P(('ctx', 'branch'), None, 'head')
- branch_kv_grad: bfloat16 [8, 128, 1024], P(('ctx', 'branch'), None, 'head')
- trunk_kv_grad: bfloat16 [192, 1024], P(('ctx', 'branch'), 'head')
Inputs may be any that keep to these rules, and one draw needn't show every extreme that they name: `block_mask`: each entry is 0 or 1; columns 0 to 1 are the trunk's blocks, the rest the branch's own blocks, of which those on or above the query block's diagonal are not read. Every query block of every branch sees at least one trunk block. The share of ones differs from branch to branch.
All inputs are finite; a program needn't handle non-finite values.
Results may differ from a plain program's by a relative error of at most 0.017.
Values may be sent and summed in bfloat16 or wider, within the bound.
No kernel may reach another device: no remote copies, remote signals or barrier semaphores. Data moves between devices by JAX's collectives and lax.ppermute only.
A program may use at most 64 MiB of HBM per device.

v0:
```python
import math
import jax
import jax.numpy as jnp
from jax import lax
from jax.sharding import PartitionSpec as P

HEAD_WIDTH = 128
BLK = 128
masked_fill = -1e30


def head_scores(query_row_block, key_row_block, score_scale):
    return (
        jnp.einsum(
            "igd,kd->gik", query_row_block, key_row_block, preferred_element_type=jnp.float32
        )
        * score_scale
    )


def block_gradients(
    query_row_block,
    gradient_rows,
    key_row_block,
    value_rows,
    allowed,
    log_total,
    out_dot,
    score_scale,
):
    scores = head_scores(query_row_block, key_row_block, score_scale)
    weights = jnp.exp(jnp.where(allowed[None], scores, masked_fill) - log_total)
    weights_low = weights.astype(jnp.bfloat16)
    grad_weights = jnp.einsum(
        "igd,kd->gik", gradient_rows, value_rows, preferred_element_type=jnp.float32
    )
    grad_scores = (weights * (grad_weights - out_dot)).astype(jnp.bfloat16)
    query_portion = jnp.einsum(
        "gik,kd->igd", grad_scores, key_row_block, preferred_element_type=jnp.float32
    )
    key_gradient = (
        jnp.einsum("gik,igd->kd", grad_scores, query_row_block, preferred_element_type=jnp.float32)
        * score_scale
    )
    value_gradient = jnp.einsum(
        "gik,igd->kd", weights_low, gradient_rows, preferred_element_type=jnp.float32
    )
    return (query_portion, jnp.concatenate([key_gradient, value_gradient], axis=1))


def trunk_allowed(trunk_mask, offset, key_count, branch_len):
    tokens = offset + jnp.arange(key_count, dtype=jnp.int32)
    blocks = jnp.arange(trunk_mask.shape[1], dtype=jnp.int32)
    onehot = (tokens[None, :] // BLK == blocks[:, None]).astype(jnp.float32)
    visible = jnp.dot(trunk_mask, onehot, preferred_element_type=jnp.float32) > 0.5
    spread = jnp.broadcast_to(visible[:, None, :], (visible.shape[0], BLK, key_count))
    return spread.reshape(branch_len, key_count)


def branch_allowed(branch_mask, branch_len):
    block_count = branch_mask.shape[0]
    spread = jnp.broadcast_to(
        branch_mask[:, None, :, None] > 0, (block_count, BLK, block_count, BLK)
    ).reshape(branch_len, branch_len)
    position = jnp.arange(branch_len, dtype=jnp.int32)
    query_block = position[:, None] // BLK
    key_block = position[None, :] // BLK
    earlier = (key_block < query_block) & spread
    causal = (key_block == query_block) & (position[None, :] <= position[:, None])
    return earlier | causal


def shards(
    queries,
    branch_keys,
    branch_value_rows,
    trunk_key_rows,
    trunk_value_rows,
    attn_out,
    out_grad,
    block_mask,
):
    branch_len = queries.shape[1]
    group_width = queries.shape[2] // HEAD_WIDTH
    score_scale = 1.0 / math.sqrt(HEAD_WIDTH)
    query_row_block = queries[0].reshape(branch_len, group_width, HEAD_WIDTH)
    gradient_rows = out_grad[0].reshape(branch_len, group_width, HEAD_WIDTH)
    output_rows = attn_out[0].reshape(branch_len, group_width, HEAD_WIDTH)
    branch_own_keys = branch_keys[0]
    branch_own_values = branch_value_rows[0]
    mask_rows = block_mask[0]
    query_blocks = branch_len // BLK
    trunk_blocks = mask_rows.shape[1] - query_blocks
    trunk_mask = mask_rows[:, :trunk_blocks].astype(jnp.float32)
    own_allowed = branch_allowed(mask_rows[:, trunk_blocks:], branch_len)
    own_scores = jnp.where(
        own_allowed[None], head_scores(query_row_block, branch_own_keys, score_scale), masked_fill
    )
    row_max = jnp.max(own_scores, axis=2, keepdims=True)
    row_total = jnp.sum(jnp.exp(own_scores - row_max), axis=2, keepdims=True)
    trunk_rows, trunk_vals = (
        lax.all_gather(trunk_key_rows, "ctx", axis=0, tiled=True),
        lax.all_gather(trunk_value_rows, "ctx", axis=0, tiled=True),
    )
    trunk_len = trunk_rows.shape[0]
    block_len = math.gcd(512, trunk_len)
    block_total = trunk_len // block_len
    key_blocks = trunk_rows.reshape(block_total, block_len, HEAD_WIDTH)
    value_blocks = trunk_vals.reshape(block_total, block_len, HEAD_WIDTH)
    offsets = jnp.arange(block_total, dtype=jnp.int32) * block_len

    def stats_step(running, inputs):
        run_max, run_total = running
        key_block, offset = inputs
        allowed = trunk_allowed(trunk_mask, offset, block_len, branch_len)
        scores = jnp.where(
            allowed[None], head_scores(query_row_block, key_block, score_scale), masked_fill
        )
        new_max = jnp.maximum(run_max, jnp.max(scores, axis=2, keepdims=True))
        new_total = run_total * jnp.exp(run_max - new_max) + jnp.sum(
            jnp.exp(scores - new_max), axis=2, keepdims=True
        )
        return ((new_max, new_total), None)

    (row_max, row_total), ignored = lax.scan(
        stats_step, (row_max, row_total), (key_blocks, offsets)
    )
    log_total = row_max + jnp.log(row_total)
    out_dot = jnp.sum(
        gradient_rows.astype(jnp.float32) * output_rows.astype(jnp.float32), axis=2
    ).T[:, :, None]
    own_query, own_grad = block_gradients(
        query_row_block,
        gradient_rows,
        branch_own_keys,
        branch_own_values,
        own_allowed,
        log_total,
        out_dot,
        score_scale,
    )

    def grad_step(query_sum, inputs):
        key_block, value_block, offset = inputs
        allowed = trunk_allowed(trunk_mask, offset, block_len, branch_len)
        query_portion, key_value_pair = block_gradients(
            query_row_block,
            gradient_rows,
            key_block,
            value_block,
            allowed,
            log_total,
            out_dot,
            score_scale,
        )
        return (query_sum + query_portion, key_value_pair)

    query_sum, trunk_grad = lax.scan(grad_step, own_query, (key_blocks, value_blocks, offsets))
    query_out = (
        (query_sum * score_scale)
        .astype(jnp.bfloat16)
        .reshape(1, branch_len, group_width * HEAD_WIDTH)
    )
    branch_out = own_grad.astype(jnp.bfloat16)[None]
    trunk_term = lax.optimization_barrier(
        trunk_grad.reshape(trunk_len, 2 * HEAD_WIDTH).astype(jnp.bfloat16)
    ).astype(jnp.float32)
    reduced = lax.psum_scatter(
        trunk_term.astype(jnp.bfloat16), "ctx", scatter_dimension=0, tiled=True
    )
    trunk_out = lax.psum_scatter(reduced, "branch", scatter_dimension=0, tiled=True).astype(
        jnp.float32
    )
    return (query_out, branch_out, trunk_out.astype(jnp.bfloat16))


def solution(mesh):
    return jax.shard_map(
        shards,
        mesh=mesh,
        in_specs=(
            P(("ctx", "branch"), None, "head"),
            P(("ctx", "branch"), None, "head"),
            P(("ctx", "branch"), None, "head"),
            P("ctx", "head"),
            P("ctx", "head"),
            P(("ctx", "branch"), None, "head"),
            P(("ctx", "branch"), None, "head"),
            P(("ctx", "branch"), None, None),
        ),
        out_specs=(
            P(("ctx", "branch"), None, "head"),
            P(("ctx", "branch"), None, "head"),
            P(("ctx", "branch"), "head"),
        ),
        check_vma=False,
    )
```

profile of v0, /device:TPU:0, one launch (start us, length us, event | category | flops | bytes accessed | tf_op | source)
XLA Modules:
  0.0 79.4 jit_solution(5890720401216771830)
XLA Ops:
  7.2 0.6 copy-done.5
  7.8 0.6 slice.6
  8.5 5.7 %all_gather.6 = bf16[192,128]{1,0:T(8,128)(2,1)S(1)} all-gather(bf16[96,128]{1,0:T(8,128)(2,1)} %param.15), channel_id=1, replica_groups=mesh['ctx'=2,'branch'=4,'head'=4] {'ctx'}, dimensions={0}, use_global_device_ids=true | all-gather | bytes 73728 | tf_op jit(solution)/shard_map/all_gather | solution.py:102
  14.2 4.5 %all_gather.7 = bf16[192,128]{1,0:T(8,128)(2,1)S(1)} all-gather(bf16[96,128]{1,0:T(8,128)(2,1)S(1)} %copy-done.4), channel_id=1, replica_groups=mesh['ctx'=2,'branch'=4,'head'=4] {'ctx'}, dimensions={0}, use_global_device_ids=true | all-gather | bytes 73728 | tf_op jit(solution)/shard_map/all_gather | solution.py:103
  18.7 1.1 %copy.19 = bf16[1,128,1024]{1,2,0:T(8,128)(2,1)S(1)} copy(bf16[1,128,1024]{2,1,0:T(8,128)(2,1)} %param.12) | data formatting | bytes 524288 | tf_op args[0]
  19.8 0.2 copy.21
  20.0 0.8 copy-done.1
  20.8 0.2 copy.24
  20.9 0.8 copy-done.2
  21.7 0.2 copy.22
  21.9 0.2 copy.28
  22.8 0.1 fusion.50
  22.9 0.2 fusion.55
  23.1 0.1 exponential_reduce_fusion.1
  23.3 5.1 %while.28 = (s32[]{:T(128)}, f32[8,128,1]{1,0,2:T(8,128)S(1)}, f32[8,128,1]{1,0,2:T(8,128)S(1)}, s32[3]{0:T(128)S(1)}, bf16[1,2]{1,0:T(2,128)(2,1)S(1)}, /*index...) while((s32[]{:T(128)}, f32[8,128,1]{1,0,2:T(8,128)S(1)}, ...), condition=%wide.region_5.6_spmd, body=%wide.region_2.5_spmd.sunk | while | flops 17108416 | bytes 857269 | solution.py:125
  23.3 0.6 dynamic_slice.57
  23.9 0.7 and_select_fusion.5
  24.5 0.1 fusion.95
  24.6 0.2 fusion.96
  25.0 0.6 dynamic_slice.57
  25.6 0.7 and_select_fusion.5
  26.2 0.1 fusion.95
  26.3 0.2 fusion.96
  26.7 0.6 dynamic_slice.57
  27.3 0.7 and_select_fusion.5
  27.9 0.1 fusion.95
  28.1 0.2 fusion.96
  28.4 0.2 fusion.39
  28.6 0.3 convolution_bitcast_fusion.6
  28.9 0.2 copy.26
  29.1 9.3 %while.29 = (s32[]{:T(128)}, f32[128,8,128]{0,2,1:T(8,128)S(1)}, bf16[3,64,256]{2,1,0:T(8,128)(2,1)}, bf16[3,64,128]{2,1,0:T(8,128)(2,1)S(1)}, s32[3]{0:T(128)S(...) while((s32[]{:T(128)}, f32[128,8,128]{0,2,1:T(8,128)S(1)}, ...), condition=%wide.region_8.9_spmd, body=%wide.region_7.8_spmd.sunk | while | flops 84559296 | bytes 3433697 | solution.py:158
  29.1 0.6 dynamic_slice.61
  29.7 0.7 and_select_fusion.6
  30.4 0.1 fusion.109
  30.5 0.2 fusion.110
  30.7 0.2 convolution_bitcast_fusion.11
  30.9 0.2 fusion.111
  31.1 0.2 fusion.113
  31.3 0.6 fusion.114
  31.9 0.3 fusion.112
  32.2 0.6 dynamic_slice.61
  32.8 0.7 and_select_fusion.6
  33.5 0.1 fusion.109
  33.6 0.2 fusion.110
  33.8 0.2 convolution_bitcast_fusion.11
  34.0 0.2 fusion.111
  34.2 0.2 fusion.113
  34.4 0.6 fusion.114
  35.0 0.3 fusion.112
  35.3 0.6 dynamic_slice.61
  35.9 0.7 and_select_fusion.6
  36.6 0.1 fusion.109
  36.7 0.2 fusion.110
  36.9 0.2 convolution_bitcast_fusion.11
  37.1 0.2 fusion.111
  37.3 0.2 fusion.113
  37.5 0.6 fusion.114
  38.1 0.3 fusion.112
  38.5 0.2 fusion.44
  38.7 0.2 fusion.43
  39.1 11.4 %reduce-scatter.3.cloned.1.call-done = bf16[96,256]{1,0:T(8,128)(2,1)} async-done(((bf16[192,256]{1,0:T(8,128)(2,1)}), bf16[96,256]{1,0:T(8,128)(2,1)}) %reduce-scatter.3.cloned.1.call-update) | async-done | bytes 49168 | tf_op jit(solution)/shard_map/reduce_scatter | solution.py:168
  50.5 0.7 copy.32
  51.2 0.8 %copy.38 = bf16[1,128,1024]{2,1,0:T(8,128)(2,1)} copy(bf16[1,128,1024]{1,2,0:T(8,128)(2,1)S(1)} %bitcast.209) | data formatting | bytes 524288 | tf_op jit(solution)/shard_map/reshape | solution.py:162
  52.1 20.5 %reduce-scatter.5.cloned.1.call-done = bf16[24,256]{1,0:T(8,128)(2,1)} async-done(((bf16[96,256]{1,0:T(8,128)(2,1)}), bf16[24,256]{1,0:T(8,128)(2,1)}) %reduce-scatter.5.cloned.1.call-update) | async-done | bytes 12304 | tf_op jit(solution)/shard_map/reduce_scatter | solution.py:171
  (33 shorter events, 0.5 us)
Async XLA Ops:
  7.2 15.7 %copy-start = (bf16[1,128,128]{2,1,0:T(8,128)(2,1)S(1)}, bf16[1,128,128]{2,1,0:T(8,128)(2,1)}, u32[]{:S(2)}) copy-start(bf16[1,128,128]{2,1,0:T(8,128)(2,1)} %param.13) | copy-start | bytes 98308
  7.2 0.7 copy-start.5
  7.2 43.2 %reduce-scatter.3.cloned.1.call-start = ((), (), s32[]{:S(2)}) async-start(), calls=%async_computation.2 | async-start | bytes 147456 | tf_op jit(solution)/shard_map/reduce_scatter | solution.py:168
  8.4 5.7 %copy-start.4 = (bf16[96,128]{1,0:T(8,128)(2,1)S(1)}, bf16[96,128]{1,0:T(8,128)(2,1)}, u32[]{:S(2)}) copy-start(bf16[96,128]{1,0:T(8,128)(2,1)} %param.16) | copy-start | bytes 73732
  19.8 1.0 %copy-start.1 = (bf16[1,128,1024]{2,1,0:T(8,128)(2,1)S(1)}, bf16[1,128,1024]{2,1,0:T(8,128)(2,1)}, u32[]{:S(2)}) copy-start(bf16[1,128,1024]{2,1,0:T(8,128)(2,1)} %param.17) | copy-start | bytes 786436
  20.8 0.9 %copy-start.2 = (bf16[1,128,1024]{2,1,0:T(8,128)(2,1)S(1)}, bf16[1,128,1024]{2,1,0:T(8,128)(2,1)}, u32[]{:S(2)}) copy-start(bf16[1,128,1024]{2,1,0:T(8,128)(2,1)} %param.18) | copy-start | bytes 786436
  23.2 5.2 %copy-start.3 = (bf16[1,128,128]{2,1,0:T(8,128)(2,1)S(1)}, bf16[1,128,128]{2,1,0:T(8,128)(2,1)}, u32[]{:S(2)}) copy-start(bf16[1,128,128]{2,1,0:T(8,128)(2,1)} %param.14) | copy-start | bytes 98308
  38.4 34.1 %reduce-scatter.5.cloned.1.call-start = ((), (), s32[]{:S(2)}) async-start(), calls=%async_computation.3 | async-start | bytes 61440 | tf_op jit(solution)/shard_map/reduce_scatter | solution.py:171
Sparse Core Ops, SparseCore 0:
  38.6 11.8 reduce-scatter.2
  53.2 19.2 reduce-scatter.4
where the time goes:
time: 79.8 us; the launch traced here: 79.4 us
  waiting for transfers between devices  31.9 us (40%)
  between operations  14.9 us (19%)
  blocking collectives  10.2 us (13%)
  local copies, waits for them, and re-layouts  9.88 us (12%)
  other arithmetic  6.35 us (8%)
  matrix products  5.74 us (7%)
    reduce_scatter x1, waiting for transfers between devices, shards(): lax.psum_scatter(reduced, 'branch', scatter_dimension=0, tiled=True)  20.5 us
    reduce_scatter x1, waiting for transfers between devices, shards(): lax.psum_scatter(trunk_term.astype(jnp.bfloat16), 'ctx', scatter_dimensio...  11.4 us
    all_gather x1, blocking collectives, shards(): lax.all_gather(trunk_key_rows, 'ctx', axis=0, tiled=True)  5.73 us
    all_gather x1, blocking collectives, shards(): lax.all_gather(trunk_value_rows, 'ctx', axis=0, tiled=True)  4.48 us
    unnamed x16, local copies, waits for them, and re-layouts  4.36 us
    select_n x6, other arithmetic, trunk_allowed(): onehot = (tokens[None, :] // BLK == blocks[:, None]).astype(jnp.float32)  3.92 us
    dynamic_slice x6, local copies, waits for them, and re-layouts, shards(): lax.scan(stats_step, (row_max, row_total), (key_blocks, offsets))  3.52 us
    dynamic_update_slice x3, other arithmetic, shards(): lax.scan(grad_step, own_query, (key_blocks, value_blocks, offsets))  1.88 us
  transfers between devices with their start and end apart: 2, of which 2 were waited for; matrix products, arithmetic and copies ran while one was open for 3% of the time, Pallas kernels for 0%

commit v1 on v0

--- a/solution.py
+++ b/solution.py
@@ -7,6 +7,18 @@
 HEAD_WIDTH = 128
 BLK = 128
 masked_fill = -1e30
+
+
+def doubled_up(value, axis, dim):
+    ways, here, lap = (lax.axis_size(axis), lax.axis_index(axis), value.shape[dim])
+    line, have = (value, 1)
+    while have < ways:
+        line = jnp.concatenate(
+            [line, lax.ppermute(line, axis, [(d, (d - have) % ways) for d in range(ways)])],
+            axis=dim,
+        )
+        have = 2 * have
+    return jnp.roll(line, here * lap, axis=dim)
 
 
 def head_scores(query_row_block, key_row_block, score_scale):
@@ -99,7 +111,7 @@
     row_max = jnp.max(own_scores, axis=2, keepdims=True)
     row_total = jnp.sum(jnp.exp(own_scores - row_max), axis=2, keepdims=True)
     trunk_rows, trunk_vals = (
-        lax.all_gather(trunk_key_rows, "ctx", axis=0, tiled=True),
+        doubled_up(trunk_key_rows, "ctx", 0),
         lax.all_gather(trunk_value_rows, "ctx", axis=0, tiled=True),
     )
     trunk_len = trunk_rows.shape[0]

time: 79.8 us -> 76.9 us (0.964)
  blocking collectives: 10.2 us -> 4.61 us
  starting transfers between devices: 0.08 us -> 3.14 us
  waiting for transfers between devices: 31.9 us -> 31 us
    all_gather x1 -> x0, blocking collectives: 5.73 us -> none  [shards(): lax.all_gather(trunk_key_rows, 'ctx', axis=0, tiled=True)]
    ppermute x0 -> x1, starting transfers between devices: none -> 3.06 us  [doubled_up(): lax.ppermute(line, axis, [(d, (d - have) % ways) for d in range(ways)])]
    reduce_scatter x1, waiting for transfers between devices: 11.4 us -> 10.5 us  [shards(): lax.psum_scatter(trunk_term.astype(jnp.bfloat16), 'ctx', scatter_dimensio...]
    unnamed x16 -> x18, local copies, waits for them, and re-layouts: 4.36 us -> 4.07 us
  transfers between devices with their start and end apart: 2 -> 3, of which waited for: 2 -> 2; matrix products, arithmetic and copies ran while one was open for 3% -> 6% of each run, Pallas kernels for 0% -> 0%
where the time goes in v1:
time: 76.9 us; the launch traced here: 76.4 us
  waiting for transfers between devices  31 us (40%)
  between operations  14.9 us (19%)
  local copies, waits for them, and re-layouts  9.82 us (13%)
  other arithmetic  6.83 us (9%)
  matrix products  5.74 us (7%)
  blocking collectives  4.61 us (6%)
  starting transfers between devices  3.14 us (4%)
    reduce_scatter x1, waiting for transfers between devices, shards(): lax.psum_scatter(reduced, 'branch', scatter_dimension=0, tiled=True)  20.5 us
    reduce_scatter x1, waiting for transfers between devices, shards(): lax.psum_scatter(trunk_term.astype(jnp.bfloat16), 'ctx', scatter_dimensio...  10.5 us
    all_gather x1, blocking collectives, shards(): lax.all_gather(trunk_value_rows, 'ctx', axis=0, tiled=True)  4.61 us
    unnamed x18, local copies, waits for them, and re-layouts  4.07 us
    select_n x6, other arithmetic, trunk_allowed(): onehot = (tokens[None, :] // BLK == blocks[:, None]).astype(jnp.float32)  4.05 us
    dynamic_slice x6, local copies, waits for them, and re-layouts, shards(): lax.scan(stats_step, (row_max, row_total), (key_blocks, offsets))  3.76 us
    ppermute x1, starting transfers between devices, doubled_up(): lax.ppermute(line, axis, [(d, (d - have) % ways) for d in range(ways)])  3.06 us
    dynamic_update_slice x3, other arithmetic, shards(): lax.scan(grad_step, own_query, (key_blocks, value_blocks, offsets))  1.88 us
  transfers between devices with their start and end apart: 3, of which 2 were waited for; matrix products, arithmetic and copies ran while one was open for 6% of the time, Pallas kernels for 0%

profile of v1, /device:TPU:0, one launch (start us, length us, event | category | flops | bytes accessed | tf_op | source)
XLA Modules:
  0.0 76.4 jit_solution(5417785233440600571)
XLA Ops:
  7.2 3.1 %collective-permute-start = (bf16[96,128]{1,0:T(8,128)(2,1)}, bf16[96,128]{1,0:T(8,128)(2,1)S(1)}, u32[]{:S(2)}, u32[]{:S(2)}) collective-permute-start(bf16[96,128]{1,0:T(8,128)(2,1)} %param.15), channel_id=1, source_target_pairs={{0,16},{16,0},{1,17},{17,1},{2,18},{18,2},{3,19},{19,3},{4,20},{20... | collective-permute-start | bytes 73736 | tf_op jit(solution)/shard_map/ppermute | solution.py:17
  10.3 0.6 slice.6
  10.9 1.2 %copy.19 = bf16[1,128,1024]{1,2,0:T(8,128)(2,1)S(1)} copy(bf16[1,128,1024]{2,1,0:T(8,128)(2,1)} %param.12) | data formatting | bytes 524288 | tf_op args[0]
  12.1 0.2 copy.24
  12.3 0.8 %copy-done.2 = bf16[1,128,1024]{2,1,0:T(8,128)(2,1)S(1)} copy-done((bf16[1,128,1024]{2,1,0:T(8,128)(2,1)S(1)}, bf16[1,128,1024]{2,1,0:T(8,128)(2,1)}, u32[]{:S(2)}) %copy-start.2) | copy-done | bytes 262168
  13.0 0.2 copy.22
  14.0 0.2 fusion.58
  14.3 0.1 exponential_reduce_fusion.1
  14.4 0.2 copy.21
  14.6 0.2 copy.28
  14.8 0.5 copy-done.4
  15.3 4.6 %all_gather.3 = bf16[192,128]{1,0:T(8,128)(2,1)S(1)} all-gather(bf16[96,128]{1,0:T(8,128)(2,1)S(1)} %copy-done.4), channel_id=1, replica_groups=mesh['ctx'=2,'branch'=4,'head'=4] {'ctx'}, dimensions={0}, use_global_device_ids=true | all-gather | bytes 73728 | tf_op jit(solution)/shard_map/all_gather | solution.py:115
  20.0 0.4 fusion.53
  20.3 5.5 %while.28 = (s32[]{:T(128)}, f32[8,128,1]{1,0,2:T(8,128)S(1)}, f32[8,128,1]{1,0,2:T(8,128)S(1)}, s32[3]{0:T(128)S(1)}, bf16[1,2]{1,0:T(2,128)(2,1)S(1)}, /*index...) while((s32[]{:T(128)}, f32[8,128,1]{1,0,2:T(8,128)S(1)}, ...), condition=%wide.region_5.6_spmd, body=%wide.region_2.5_spmd.sunk | while | flops 17108416 | bytes 857269 | solution.py:137
  20.3 0.7 dynamic_slice.82
  21.0 0.7 and_select_fusion.5
  21.7 0.1 fusion.98
  21.8 0.2 fusion.99
  22.2 0.7 dynamic_slice.82
  22.8 0.7 and_select_fusion.5
  23.5 0.1 fusion.98
  23.7 0.2 fusion.99
  24.0 0.7 dynamic_slice.82
  24.7 0.7 and_select_fusion.5
  25.4 0.1 fusion.98
  25.5 0.2 fusion.99
  25.9 0.2 fusion.44
  26.1 0.5 copy-done.3
  26.6 0.2 fusion.39
  26.8 0.2 fusion.43
  27.1 0.3 convolution_bitcast_fusion.6
  27.3 0.2 copy.26
  27.5 9.3 %while.29 = (s32[]{:T(128)}, f32[128,8,128]{0,2,1:T(8,128)S(1)}, bf16[3,64,256]{2,1,0:T(8,128)(2,1)}, bf16[3,64,128]{2,1,0:T(8,128)(2,1)S(1)}, s32[3]{0:T(128)S(...) while((s32[]{:T(128)}, f32[128,8,128]{0,2,1:T(8,128)S(1)}, ...), condition=%wide.region_8.9_spmd, body=%wide.region_7.8_spmd.sunk | while | flops 84559296 | bytes 3433697 | solution.py:170
  27.5 0.6 dynamic_slice.86
  28.1 0.7 and_select_fusion.6
  28.8 0.1 fusion.112
  28.9 0.2 fusion.113
  29.1 0.2 convolution_bitcast_fusion.11
  29.3 0.2 fusion.114
  29.5 0.2 fusion.116
  29.7 0.6 fusion.117
  30.4 0.3 fusion.115
  30.6 0.6 dynamic_slice.86
  31.2 0.7 and_select_fusion.6
  31.9 0.1 fusion.112
  32.0 0.2 fusion.113
  32.2 0.2 convolution_bitcast_fusion.11
  32.4 0.2 fusion.114
  32.6 0.2 fusion.116
  32.8 0.6 fusion.117
  33.5 0.3 fusion.115
  33.7 0.6 dynamic_slice.86
  34.3 0.7 and_select_fusion.6
  35.0 0.1 fusion.112
  35.1 0.2 fusion.113
  35.3 0.2 convolution_bitcast_fusion.11
  35.5 0.2 fusion.114
  35.8 0.2 fusion.116
  35.9 0.6 fusion.117
  36.6 0.3 fusion.115
  37.0 10.5 %reduce-scatter.3.cloned.1.call-done = bf16[96,256]{1,0:T(8,128)(2,1)} async-done(((bf16[192,256]{1,0:T(8,128)(2,1)}), bf16[96,256]{1,0:T(8,128)(2,1)}) %reduce-scatter.3.cloned.1.call-update) | async-done | bytes 49168 | tf_op jit(solution)/shard_map/reduce_scatter | solution.py:180
  47.5 0.7 copy.32
  48.2 0.8 %copy.38 = bf16[1,128,1024]{2,1,0:T(8,128)(2,1)} copy(bf16[1,128,1024]{1,2,0:T(8,128)(2,1)S(1)} %bitcast.209) | data formatting | bytes 524288 | tf_op jit(solution)/shard_map/reshape | solution.py:174
  49.1 20.5 %reduce-scatter.5.cloned.1.call-done = bf16[24,256]{1,0:T(8,128)(2,1)} async-done(((bf16[96,256]{1,0:T(8,128)(2,1)}), bf16[24,256]{1,0:T(8,128)(2,1)}) %reduce-scatter.5.cloned.1.call-update) | async-done | bytes 12304 | tf_op jit(solution)/shard_map/reduce_scatter | solution.py:183
  (37 shorter events, 0.6 us)
Async XLA Ops:
  7.2 6.9 %copy-start = (bf16[1,128,128]{2,1,0:T(8,128)(2,1)S(1)}, bf16[1,128,128]{2,1,0:T(8,128)(2,1)}, u32[]{:S(2)}) copy-start(bf16[1,128,128]{2,1,0:T(8,128)(2,1)} %param.13) | copy-start | bytes 98308
  7.2 3.1 %copy-start.6 = (s32[1,1,3]{2,1,0:T(1,128)S(1)}, s32[1,1,3]{2,1,0:T(1,128)}, u32[]{:S(2)}) copy-start(s32[1,1,3]{2,1,0:T(1,128)} %param.19) | copy-start | bytes 40
  7.2 40.3 %reduce-scatter.3.cloned.1.call-start = ((), (), s32[]{:S(2)}) async-start(), calls=%async_computation.2 | async-start | bytes 147456 | tf_op jit(solution)/shard_map/reduce_scatter | solution.py:180
  7.2 12.7 %collective-permute-start = (bf16[96,128]{1,0:T(8,128)(2,1)}, bf16[96,128]{1,0:T(8,128)(2,1)S(1)}, u32[]{:S(2)}, u32[]{:S(2)}) collective-permute-start(bf16[96,128]{1,0:T(8,128)(2,1)} %param.15), channel_id=1, source_target_pairs={{0,16},{16,0},{1,17},{17,1},{2,18},{18,2},{3,19},{19,3},{4,20},{20... | collective-permute-start | bytes 73736 | tf_op jit(solution)/shard_map/ppermute | solution.py:17
  10.9 1.2 %copy-start.1 = (bf16[1,128,1024]{2,1,0:T(8,128)(2,1)S(1)}, bf16[1,128,1024]{2,1,0:T(8,128)(2,1)}, u32[]{:S(2)}) copy-start(bf16[1,128,1024]{2,1,0:T(8,128)(2,1)} %param.17) | copy-start | bytes 786436
  12.1 1.0 %copy-start.2 = (bf16[1,128,1024]{2,1,0:T(8,128)(2,1)S(1)}, bf16[1,128,1024]{2,1,0:T(8,128)(2,1)}, u32[]{:S(2)}) copy-start(bf16[1,128,1024]{2,1,0:T(8,128)(2,1)} %param.18) | copy-start | bytes 786436
  14.6 0.7 copy-start.4
  15.3 4.6 %copy-start.5 = (bf16[96,128]{1,0:T(8,128)(2,1)S(1)}, bf16[96,128]{1,0:T(8,128)(2,1)}, u32[]{:S(2)}) copy-start(bf16[96,128]{1,0:T(8,128)(2,1)} %param.15) | copy-start | bytes 73732
  25.8 0.8 copy-start.3
  36.9 32.7 %reduce-scatter.5.cloned.1.call-start = ((), (), s32[]{:S(2)}) async-start(), calls=%async_computation.3 | async-start | bytes 61440 | tf_op jit(solution)/shard_map/reduce_scatter | solution.py:183
Sparse Core Ops, SparseCore 0:
  37.0 10.4 reduce-scatter.2
  50.3 19.2 reduce-scatter.4
